TPU v7x, 768 devices: a whole 4x8x12 slice. The times are simulated.
768 devices in a mesh: section: 48 (over y_lo, z, core), tensor: 4 (over y_hi), dp: 4 (over x).
Axes of the slice: x: 4, y: 8 (y_hi: 4, y_lo: 2; y = y_hi * 2 + y_lo), z: 12, core: 2. Of those that a mesh axis runs over, the one named last changes fastest.
Arguments:
- hidden: bfloat16 [1536, 8192], P(('section', 'dp'), 'tensor'), may hold values from -250 to 250
- vocab_weight: bfloat16 [8192, 122880], P(None, ('section', 'tensor')), may hold values from -0.6 to 0.6
- target_ids: int32 [1536], P(('section', 'dp')), may hold values from 0 to 122879
- ref_logp: float32 [1536], P(('section', 'dp')), may hold values from -8 to -0.5
- response_lengths: int32 [192], P(('section', 'dp')), may hold values from 1 to 8
Outputs:
- token_logp: float32 [1536], P(('section', 'dp'))
- entropy: float32 [1536], P(('section', 'dp'))
- kl_term: float32 [1536], P(('section', 'dp'))
All inputs are finite; a program needn't handle non-finite values.
Results may differ from a plain program's by a relative error of at most 0.0015.
Values may be sent and summed in bfloat16 or wider, within the bound.
No kernel may reach another device: no remote copies, remote signals or barrier semaphores. Data moves between devices by JAX's collectives and lax.ppermute only.
A program may use at most 64 MiB of HBM per device.

v0:
```python
import functools

import jax
import jax.numpy as jnp
from jax import lax
from jax.experimental import pallas as pl
from jax.experimental.pallas import tpu as pltpu
from jax.sharding import Mesh, PartitionSpec as P

NY, NZ, NR = 8, 12, 3
NQ = NZ // NR
LANES = 128
CHUNK = 1024
PLANE = ("y_lo", "zq", "zr", "core", "tensor")


def place(y, z, core):
    y, z = y % NY, z % NZ
    return ((y % 2) * NZ * 2 + z * 2 + core) * (NY // 2) + y // 2


def fetch(x, source):
    pairs = [
        (place(*source(y, z, c)), place(y, z, c))
        for y in range(NY)
        for z in range(NZ)
        for c in range(2)
    ]
    return lax.ppermute(x, PLANE, pairs)


def above(y, z, c):
    return y, z + 1, c


def below(y, z, c):
    return y, z - 1, c


def across(y, z, c):
    return y + 1 - 2 * c, z, c


def partner(y, z, c):
    return y, z, 1 - c


def stats_kernel(pieces, chunk, offset_ref, *refs):
    rows, (w_ref, out_ref, acc) = refs[:pieces], refs[pieces:]
    depth = w_ref.shape[0]
    for k in range(depth // chunk):
        x = jnp.concatenate([r[:, k * chunk : (k + 1) * chunk] for r in rows], axis=0)
        part = jnp.dot(x, w_ref[k * chunk : (k + 1) * chunk, :], preferred_element_type=jnp.float32)
        if k == 0:
            acc[...] = part
        else:
            acc[...] += part
    logits = acc[...]
    digits = jnp.concatenate([r[:, depth:] for r in rows], axis=0).astype(jnp.float32)
    ids = (digits[:, 2:3] * 256 + digits[:, 1:2]) * 256 + digits[:, 0:1]
    column = lax.broadcasted_iota(jnp.int32, logits.shape, 1) + offset_ref[0]
    top = jnp.max(logits, axis=1, keepdims=True)
    expo = jnp.exp(logits - top)
    total = jnp.sum(expo, axis=1, keepdims=True)
    moment = jnp.sum(expo * logits, axis=1, keepdims=True)
    hit = column == ids.astype(jnp.int32)
    picked = jnp.sum(jnp.where(hit, logits, 0.0), axis=1, keepdims=True)
    lane = lax.broadcasted_iota(jnp.int32, out_ref.shape, 1)
    low = jnp.where(lane == 0, top, total)
    high = jnp.where(lane == 2, moment, picked)
    out_ref[...] = jnp.where(lane < 2, low, high)


def stats_of(rows, weight, offset):
    count = sum(r.shape[0] for r in rows)
    depth, voc_dev = weight.shape
    return pl.pallas_call(
        functools.partial(stats_kernel, len(rows), CHUNK),
        out_shape=jax.ShapeDtypeStruct((count, LANES), jnp.float32),
        in_specs=[pl.BlockSpec(memory_space=pltpu.SMEM)]
        + [pl.BlockSpec(memory_space=pltpu.VMEM)] * (len(rows) + 1),
        out_specs=pl.BlockSpec(memory_space=pltpu.VMEM),
        scratch_shapes=[
            pltpu.VMEM((count, voc_dev), jnp.float32),
        ],
        compiler_params=pltpu.CompilerParams(vmem_limit_bytes=16 * 2**20),
        cost_estimate=pl.CostEstimate(
            flops=2 * count * depth * voc_dev,
            bytes_accessed=2 * depth * (count + voc_dev),
            transcendentals=count * voc_dev,
        ),
    )(offset, *rows, weight)


def per_device(hidden, vocab_weight, target_ids, ref_logp, response_lengths):
    row_dev, feat = hidden.shape
    voc_dev = vocab_weight.shape[1]
    y_lo, y_hi = lax.axis_index("y_lo"), lax.axis_index("tensor")
    core = lax.axis_index("core")
    z = lax.axis_index("zq") * NR + lax.axis_index("zr")
    section = (y_lo * NZ + z) * 2 + core
    n_sec, n_ten = 4 * NZ, NY // 2
    offset = ((section * n_ten + y_hi) * voc_dev).reshape(1).astype(jnp.int32)

    digits = jnp.stack([target_ids % 256, (target_ids // 256) % 256, target_ids // 65536], axis=1)
    digits = jnp.pad(digits.astype(jnp.bfloat16), ((0, 0), (0, LANES - 3)))
    block = jnp.concatenate([hidden, digits], axis=1)
    block = jnp.broadcast_to(block[None], (NQ * n_ten,) + block.shape)
    block = lax.all_to_all(block, ("zq", "tensor"), 0, 0)
    block = block.reshape(NQ, n_ten, row_dev, feat + LANES)
    pieces = [block[:, h, :, :feat] for h in range(n_ten)] + [block[:, 0, :, feat:]]
    unit = NQ * row_dev
    near = jnp.concatenate(pieces, axis=2).reshape(unit, n_ten * feat + LANES)

    up = fetch(near, above)
    down = fetch(near, below)
    side = fetch(near, across)
    side_up = jnp.where(core == 0, side, up)
    side_up = fetch(side_up, lambda y, z, c: (across if c else above)(y, z, c))
    side_down = jnp.where(core == 0, down, side)
    side_down = fetch(side_down, lambda y, z, c: (below if c else across)(y, z, c))
    early = jnp.concatenate([near, up, down, side], axis=0)
    early_p = fetch(early, partner)
    late = jnp.concatenate([side_up, side_down], axis=0)
    late_p = fetch(late, partner)
    stats_o = stats_of([near], vocab_weight, offset)
    stats_a = stats_of([up, down, side], vocab_weight, offset)
    stats_b = stats_of([early_p], vocab_weight, offset)
    stats_c = stats_of([late, late_p], vocab_weight, offset)

    s = jnp.arange(n_sec, dtype=jnp.int32)
    s_core, s_z, s_y = s % 2, (s // 2) % NZ, s // (2 * NZ)
    theirs = (s_core != core).astype(jnp.int32)
    unit = jnp.where(s_y == y_lo, 0, NR) + (s_z - z) % NR
    first = jnp.where(unit < 4, 4 * theirs + unit, 4 + 2 * theirs + unit)
    group = first * NQ + s_z // NR
    stats = jnp.concatenate([x[:, :4] for x in (stats_o, stats_a, stats_b, stats_c)], axis=0)
    stats = stats.reshape(n_sec, 4 * row_dev)
    choose = (group[:, None] == s[None, :]).astype(jnp.float32)
    stats = jnp.dot(choose, stats, precision=lax.Precision.HIGHEST)
    send = jnp.broadcast_to(stats[:, None, :], (n_sec, n_ten, 4 * row_dev))
    send = send.reshape(n_sec * n_ten, 1, 4 * row_dev)
    got = lax.all_to_all(send, PLANE, 0, 0).reshape(n_sec * n_ten, row_dev, 4)

    tops = got[:, :, 0]
    top = jnp.max(tops, axis=0)
    scale = jnp.exp(tops - top[None])
    total = jnp.sum(got[:, :, 1] * scale, axis=0)
    moment = jnp.sum(got[:, :, 2] * scale, axis=0)
    picked = jnp.sum(got[:, :, 3], axis=0)
    lse = top + jnp.log(total)
    logp = picked - lse
    ent = lse - moment / total
    slot = jnp.arange(row_dev, dtype=jnp.int32)
    live = (slot < response_lengths[0]).astype(jnp.float32)
    return (logp * live, ent * live, (logp - ref_logp) * live)


def solution(mesh):
    tensor, dp = mesh.shape["tensor"], mesh.shape["dp"]
    mesh = Mesh(
        mesh.devices.reshape(2, NQ, NR, 2, tensor, dp), ("y_lo", "zq", "zr", "core", "tensor", "dp")
    )
    section = ("y_lo", "zq", "zr", "core")
    rows = P(section + ("dp",))
    in_specs = (P(section + ("dp",), "tensor"), P(None, section + ("tensor",)), rows, rows, rows)
    return jax.shard_map(
        per_device, mesh=mesh, in_specs=in_specs, out_specs=(rows, rows, rows), check_vma=False
    )
```

profile of v0, /device:TPU:1, one launch (start us, length us, event | category | flops | bytes accessed | tf_op | source)
XLA Modules:
  0.0 133.4 jit_solution(15074221036783647975)
XLA Ops:
  0.6 0.7 fusion.20
  1.3 0.1 copy.37
  1.4 0.8 fusion.5
  2.2 39.8 %all_to_all.10 = bf16[16,8,2176]{2,1,0:T(8,128)(2,1)S(1)} all-to-all(bf16[16,8,2176]{2,1,0:T(8,128)(2,1)S(1)} %broadcast_in_dim.11), channel_id=1, replica_groups=mesh['y_lo'=2,'zq'=4,'zr'=3,'core'=2,'tensor'=4,'dp'=4] {'zq','tensor'}, dimensions={0} | all-to-all | bytes 1114112 | tf_op jit(solution)/shard_map/all_to_all | solution.py:109
  42.2 2.0 %collective-permute-start.2 = (bf16[32,8320]{1,0:T(8,128)(2,1)S(1)}, bf16[32,8320]{1,0:T(8,128)(2,1)S(1)}, u32[]{:S(2)}, u32[]{:S(2)}) collective-permute-start(bf16[32,8320]{1,0:T(8,128)(2,1)S(1)} %constant_dynamic-update-slice_fusion.refs_0_), channel_id=1, source_target_pairs={{384,0},{412,16},{416,32},{444,48},{448,64},{476,80},{480,96},{508... | collective-permute-start | bytes 1597448 | tf_op jit(solution)/shard_map/ppermute | solution.py:29
  44.1 13.6 %collective-permute-start.1 = (bf16[32,8320]{1,0:T(8,128)(2,1)S(1)}, bf16[32,8320]{1,0:T(8,128)(2,1)S(1)}, u32[]{:S(2)}, u32[]{:S(2)}) collective-permute-start(bf16[32,8320]{1,0:T(8,128)(2,1)S(1)} %constant_dynamic-update-slice_fusion.refs_0_), channel_id=1, source_target_pairs={{352,0},{368,16},{0,32},{16,48},{32,64},{48,80},{64,96},{80,112},{... | collective-permute-start | bytes 1597448 | tf_op jit(solution)/shard_map/ppermute | solution.py:29
  57.7 1.9 %collective-permute-start = (bf16[32,8320]{1,0:T(8,128)(2,1)S(1)}, bf16[32,8320]{1,0:T(8,128)(2,1)S(1)}, u32[]{:S(2)}, u32[]{:S(2)}) collective-permute-start(bf16[32,8320]{1,0:T(8,128)(2,1)S(1)} %constant_dynamic-update-slice_fusion.refs_0_), channel_id=1, source_target_pairs={{32,0},{48,16},{64,32},{80,48},{96,64},{112,80},{128,96},{144,112}... | collective-permute-start | bytes 1597448 | tf_op jit(solution)/shard_map/ppermute | solution.py:29
  59.7 0.0 collective-permute-done.2.refs_2_
  59.7 8.5 %collective-permute-done.1.refs_1_ = bf16[32,8320]{1,0:T(8,128)(2,1)S(1)} collective-permute-done((bf16[32,8320]{1,0:T(8,128)(2,1)S(1)}, bf16[32,8320]{1,0:T(8,128)(2,1)S(1)}, u32[]{:S(2)}, u32[]{:S(2)}) %collective-permute-start.1) | collective-permute-done | bytes 532512 | tf_op jit(solution)/shard_map/ppermute | solution.py:29
  68.2 3.8 %collective-permute-done.refs_0_ = bf16[32,8320]{1,0:T(8,128)(2,1)S(1)} collective-permute-done((bf16[32,8320]{1,0:T(8,128)(2,1)S(1)}, bf16[32,8320]{1,0:T(8,128)(2,1)S(1)}, u32[]{:S(2)}, u32[]{:S(2)}) %collective-permute-start) | collective-permute-done | bytes 532512 | tf_op jit(solution)/shard_map/ppermute | solution.py:29
  72.0 0.1 broadcast_select_fusion
  72.1 2.0 %collective-permute-start.5 = (bf16[32,8320]{1,0:T(8,128)(2,1)S(1)}, bf16[32,8320]{1,0:T(8,128)(2,1)S(1)}, u32[]{:S(2)}, u32[]{:S(2)}) collective-permute-start(bf16[32,8320]{1,0:T(8,128)(2,1)S(1)} %get-tuple-element.7), channel_id=1, source_target_pairs={{384,0},{368,16},{416,32},{16,48},{448,64},{48,80},{480,96},{80,11... | collective-permute-start | bytes 1597448 | tf_op jit(solution)/shard_map/ppermute | solution.py:29
  74.1 1.9 %collective-permute-start.4 = (bf16[32,8320]{1,0:T(8,128)(2,1)S(1)}, bf16[32,8320]{1,0:T(8,128)(2,1)S(1)}, u32[]{:S(2)}, u32[]{:S(2)}) collective-permute-start(bf16[32,8320]{1,0:T(8,128)(2,1)S(1)} %get-tuple-element.8), channel_id=1, source_target_pairs={{32,0},{412,16},{64,32},{444,48},{96,64},{476,80},{128,96},{508,11... | collective-permute-start | bytes 1597448 | tf_op jit(solution)/shard_map/ppermute | solution.py:29
  76.1 1.5 %pad_maximum_fusion = bf16[128,8320]{1,0:T(8,128)(2,1)} fusion(bf16[32,8320]{1,0:T(8,128)(2,1)S(1)} %collective-permute-done.2.refs_2_, bf16[32,8320]{1,0:T(8,128)(2,1)S(1)} %collective-permute-done.1.refs_1_, bf16[32,8320]{1,0:T(8,128)(2,1)S(1)} %collective-permute-done.refs_0_, bf16[32,8320]{1,0:T(8,128)(2,1)S(1)} %constant_dynamic-update-slice_fusion.refs_0_), kind=kLoop, calls=%fused_computation | loop fusion | flops 8519680 | bytes 4259840 | tf_op jit(solution)/shard_map/concatenate | solution.py:122
  77.6 8.0 %collective-permute-start.3 = (bf16[128,8320]{1,0:T(8,128)(2,1)}, bf16[128,8320]{1,0:T(8,128)(2,1)}, u32[]{:S(2)}, u32[]{:S(2)}) collective-permute-start(bf16[128,8320]{1,0:T(8,128)(2,1)} %pad_maximum_fusion), channel_id=1, source_target_pairs={{16,0},{0,16},{48,32},{32,48},{80,64},{64,80},{112,96},{96,112},{1... | collective-permute-start | bytes 6389768 | tf_op jit(solution)/shard_map/ppermute | solution.py:29
  85.6 0.7 collective-permute-done.4
  86.3 0.0 collective-permute-done.5
  86.4 5.5 %collective-permute-start.6 = (bf16[64,8320]{1,0:T(8,128)(2,1)S(1)}, bf16[64,8320]{1,0:T(8,128)(2,1)}, u32[]{:S(2)}, u32[]{:S(2)}) collective-permute-start(bf16[64,8320]{1,0:T(8,128)(2,1)S(1)} %constant_dynamic-update-slice_fusion.1.refs_0_), channel_id=1, source_target_pairs={{16,0},{0,16},{48,32},{32,48},{80,64},{64,80},{112,96},{96,112},{1... | collective-permute-start | bytes 3194888 | tf_op jit(solution)/shard_map/ppermute | solution.py:29
  92.0 0.0 copy-start
  92.0 4.0 %copy-done = bf16[8192,640]{1,0:T(8,128)(2,1)S(1)} copy-done((bf16[8192,640]{1,0:T(8,128)(2,1)S(1)}, bf16[8192,640]{1,0:T(8,128)(2,1)}, u32[]{:S(2)}) %copy-start) | copy-done | bytes 10485784
  96.0 0.0 slice-start
  96.0 0.0 slice-start.1
  96.0 2.1 %shard_map.76 = f32[32,128]{1,0:T(8,128)S(1)} custom-call(s32[1]{0:T(128)} %bitcast.1.offset_ref, bf16[32,8320]{1,0:T(8,128)(2,1)S(1)} %constant_dynamic-update-slice_fusion.refs_0_, bf16[8192,640]{1,0:T(8,128)(2,1)S(1)} %copy-done), custom_call_target="tpu_custom_call" | custom-call | flops 335544320 | bytes 11010048 | tf_op jit(solution)/shard_map/pallas_call | solution.py:77
  98.1 0.0 slice-start.2
  98.1 2.1 %shard_map.77 = f32[96,128]{1,0:T(8,128)S(1)} custom-call(s32[1]{0:T(128)} %bitcast.1.offset_ref, bf16[32,8320]{1,0:T(8,128)(2,1)S(1)} %collective-permute-done.refs_0_, bf16[32,8320]{1,0:T(8,128)(2,1)S(1)} %collective-permute-done.1.refs_1_, bf16[32,8320]{1,0:T(8,128)(2,1)S(1)} %collective-permute-done.2.refs_2_, bf16[8192,640]{1,0:T(8,128)(2,1)S(1)} %copy-done), custom_call_target="tpu_custom_call" | custom-call | flops 1006632960 | bytes 12058624 | tf_op jit(solution)/shard_map/pallas_call | solution.py:77
  100.2 0.0 collective-permute-done.6.refs_1_
  100.3 0.0 slice-done
  100.3 0.0 slice-done.1
  100.3 0.0 slice-done.2
  100.3 3.3 %shard_map.79 = f32[128,128]{1,0:T(8,128)S(1)} custom-call(s32[1]{0:T(128)} %bitcast.1.offset_ref, bf16[64,8320]{1,0:T(8,128)(2,1)S(1)} %constant_dynamic-update-slice_fusion.1.refs_0_, bf16[64,8320]{1,0:T(8,128)(2,1)} %collective-permute-done.6.refs_1_, bf16[8192,640]{1,0:T(8,128)(2,1)S(1)} %bitcast.59), custom_call_target="tpu_custom_call" | custom-call | flops 1342177280 | bytes 12582912 | tf_op jit(solution)/shard_map/pallas_call | solution.py:77
  103.6 0.0 copy-start.1
  103.6 0.0 collective-permute-done.3.refs_0_
  103.6 3.7 %shard_map.78 = f32[128,128]{1,0:T(8,128)S(1)} custom-call(s32[1]{0:T(128)} %bitcast.1.offset_ref, bf16[128,8320]{1,0:T(8,128)(2,1)} %collective-permute-done.3.refs_0_, bf16[8192,640]{1,0:T(8,128)(2,1)S(1)} %bitcast.59), custom_call_target="tpu_custom_call" | custom-call | flops 1342177280 | bytes 12582912 | tf_op jit(solution)/shard_map/pallas_call | solution.py:77
  107.4 0.1 reshape.99
  107.5 0.2 fusion.6
  107.7 0.7 broadcast_in_dim.12
  108.3 8.3 %all-to-all-start.1 = ((f32[192,1,32]{2,1,0:T(1,128)}), f32[192,1,32]{2,1,0:T(1,128)S(1)}, u32[]{:S(2)}, u32[]{:S(2)}) async-start(f32[192,1,32]{2,1,0:T(1,128)} %bitcast.12), calls=%async_computation.1 | async-start | bytes 196608 | tf_op jit(solution)/shard_map/all_to_all | solution.py:143
  117.3 15.1 %all-to-all-done.1 = f32[192,1,32]{2,1,0:T(1,128)S(1)} async-done(((f32[192,1,32]{2,1,0:T(1,128)}), f32[192,1,32]{2,1,0:T(1,128)S(1)}, u32[]{:S(2)}, u32[]{:S(2)}) %all-to-all-start.1) | async-done | bytes 24608 | tf_op jit(solution)/shard_map/all_to_all | solution.py:143
  132.4 0.1 copy.31
  132.5 0.2 fusion.26
  132.7 0.2 fusion.10
  132.9 0.0 copy-done.1
  132.9 0.5 subtract_select_fusion
  (13 shorter events, 0.3 us)
Async XLA Ops:
  42.2 17.5 %collective-permute-start.2 = (bf16[32,8320]{1,0:T(8,128)(2,1)S(1)}, bf16[32,8320]{1,0:T(8,128)(2,1)S(1)}, u32[]{:S(2)}, u32[]{:S(2)}) collective-permute-start(bf16[32,8320]{1,0:T(8,128)(2,1)S(1)} %constant_dynamic-update-slice_fusion.refs_0_), channel_id=1, source_target_pairs={{384,0},{412,16},{416,32},{444,48},{448,64},{476,80},{480,96},{508... | collective-permute-start | bytes 1597448 | tf_op jit(solution)/shard_map/ppermute | solution.py:29
  44.1 24.0 %collective-permute-start.1 = (bf16[32,8320]{1,0:T(8,128)(2,1)S(1)}, bf16[32,8320]{1,0:T(8,128)(2,1)S(1)}, u32[]{:S(2)}, u32[]{:S(2)}) collective-permute-start(bf16[32,8320]{1,0:T(8,128)(2,1)S(1)} %constant_dynamic-update-slice_fusion.refs_0_), channel_id=1, source_target_pairs={{352,0},{368,16},{0,32},{16,48},{32,64},{48,80},{64,96},{80,112},{... | collective-permute-start | bytes 1597448 | tf_op jit(solution)/shard_map/ppermute | solution.py:29
  57.7 14.3 %collective-permute-start = (bf16[32,8320]{1,0:T(8,128)(2,1)S(1)}, bf16[32,8320]{1,0:T(8,128)(2,1)S(1)}, u32[]{:S(2)}, u32[]{:S(2)}) collective-permute-start(bf16[32,8320]{1,0:T(8,128)(2,1)S(1)} %constant_dynamic-update-slice_fusion.refs_0_), channel_id=1, source_target_pairs={{32,0},{48,16},{64,32},{80,48},{96,64},{112,80},{128,96},{144,112}... | collective-permute-start | bytes 1597448 | tf_op jit(solution)/shard_map/ppermute | solution.py:29
  72.1 14.2 %collective-permute-start.5 = (bf16[32,8320]{1,0:T(8,128)(2,1)S(1)}, bf16[32,8320]{1,0:T(8,128)(2,1)S(1)}, u32[]{:S(2)}, u32[]{:S(2)}) collective-permute-start(bf16[32,8320]{1,0:T(8,128)(2,1)S(1)} %get-tuple-element.7), channel_id=1, source_target_pairs={{384,0},{368,16},{416,32},{16,48},{448,64},{48,80},{480,96},{80,11... | collective-permute-start | bytes 1597448 | tf_op jit(solution)/shard_map/ppermute | solution.py:29
  74.1 12.2 %collective-permute-start.4 = (bf16[32,8320]{1,0:T(8,128)(2,1)S(1)}, bf16[32,8320]{1,0:T(8,128)(2,1)S(1)}, u32[]{:S(2)}, u32[]{:S(2)}) collective-permute-start(bf16[32,8320]{1,0:T(8,128)(2,1)S(1)} %get-tuple-element.8), channel_id=1, source_target_pairs={{32,0},{412,16},{64,32},{444,48},{96,64},{476,80},{128,96},{508,11... | collective-permute-start | bytes 1597448 | tf_op jit(solution)/shard_map/ppermute | solution.py:29
  77.6 26.1 %collective-permute-start.3 = (bf16[128,8320]{1,0:T(8,128)(2,1)}, bf16[128,8320]{1,0:T(8,128)(2,1)}, u32[]{:S(2)}, u32[]{:S(2)}) collective-permute-start(bf16[128,8320]{1,0:T(8,128)(2,1)} %pad_maximum_fusion), channel_id=1, source_target_pairs={{16,0},{0,16},{48,32},{32,48},{80,64},{64,80},{112,96},{96,112},{1... | collective-permute-start | bytes 6389768 | tf_op jit(solution)/shard_map/ppermute | solution.py:29
  86.4 13.8 %collective-permute-start.6 = (bf16[64,8320]{1,0:T(8,128)(2,1)S(1)}, bf16[64,8320]{1,0:T(8,128)(2,1)}, u32[]{:S(2)}, u32[]{:S(2)}) collective-permute-start(bf16[64,8320]{1,0:T(8,128)(2,1)S(1)} %constant_dynamic-update-slice_fusion.1.refs_0_), channel_id=1, source_target_pairs={{16,0},{0,16},{48,32},{32,48},{80,64},{64,80},{112,96},{96,112},{1... | collective-permute-start | bytes 3194888 | tf_op jit(solution)/shard_map/ppermute | solution.py:29
  92.0 4.0 %copy-start = (bf16[8192,640]{1,0:T(8,128)(2,1)S(1)}, bf16[8192,640]{1,0:T(8,128)(2,1)}, u32[]{:S(2)}) copy-start(bf16[8192,640]{1,0:T(8,128)(2,1)} %refs_2_.1) | copy-start | bytes 31457284
  96.0 4.3 %slice-start = ((s8[10485760]{0:T(1024)(128)(4,1)}), s8[4194304]{0:T(1024)(128)(4,1)S(1)}, s32[]{:S(2)}) async-start(s8[10485760]{0:T(1024)(128)(4,1)} %bitcast.58), calls=%async_computation.2 | async-start | bytes 8388608
  96.0 4.3 %slice-start.1 = ((s8[10485760]{0:T(1024)(128)(4,1)}), s8[4194304]{0:T(1024)(128)(4,1)S(1)}, s32[]{:S(2)}) async-start(s8[10485760]{0:T(1024)(128)(4,1)} %bitcast.58), calls=%async_computation.3 | async-start | bytes 8388608
  98.1 2.2 %slice-start.2 = ((s8[10485760]{0:T(1024)(128)(4,1)}), s8[2097152]{0:T(1024)(128)(4,1)S(1)}, s32[]{:S(2)}) async-start(s8[10485760]{0:T(1024)(128)(4,1)} %bitcast.58), calls=%async_computation.4 | async-start | bytes 4194304
  103.6 29.2 %copy-start.1 = (f32[8]{0:T(128)S(1)}, f32[8]{0:T(128)}, u32[]{:S(2)}) copy-start(f32[8]{0:T(128)} %param.8) | copy-start | bytes 100
  108.3 24.1 %all-to-all-start.1 = ((f32[192,1,32]{2,1,0:T(1,128)}), f32[192,1,32]{2,1,0:T(1,128)S(1)}, u32[]{:S(2)}, u32[]{:S(2)}) async-start(f32[192,1,32]{2,1,0:T(1,128)} %bitcast.12), calls=%async_computation.1 | async-start | bytes 196608 | tf_op jit(solution)/shard_map/all_to_all | solution.py:143
where the time goes:
time: 134 us; the launch traced here: 133 us
  starting transfers between devices  43.2 us (32%)
  blocking collectives  39.8 us (30%)
  waiting for transfers between devices  28.2 us (21%)
  Pallas kernels  11.2 us (8%)
  local copies, waits for them, and re-layouts  5.14 us (4%)
  other arithmetic  3.98 us (3%)
  between operations  1.59 us (1%)
    all_to_all x1, blocking collectives, per_device(): block = lax.all_to_all(block, ('zq', 'tensor'), 0, 0)  39.8 us
    ppermute x7, starting transfers between devices, fetch(): return lax.ppermute(x, PLANE, pairs)  34.9 us
    all_to_all x1, waiting for transfers between devices, per_device(): got = lax.all_to_all(send, PLANE, 0, 0).reshape(n_sec * n_ten, row_dev, 4)  15.1 us
    ppermute x7, waiting for transfers between devices, fetch(): return lax.ppermute(x, PLANE, pairs)  13.1 us
    pallas_call x4, Pallas kernels, stats_of(): pl.pallas_call(functools.partial(stats_kernel, len(rows), CHUNK), out_sha...  11.2 us
    all_to_all x1, starting transfers between devices, per_device(): got = lax.all_to_all(send, PLANE, 0, 0).reshape(n_sec * n_ten, row_dev, 4)  8.29 us
    unnamed x16, local copies, waits for them, and re-layouts  4.19 us
  transfers between devices with their start and end apart: 8, of which 4 were waited for; matrix products, arithmetic and copies ran while one was open for 1% of the time, Pallas kernels for 6%

commit v1 on v0

--- a/solution.py
+++ b/solution.py
@@ -136,10 +136,8 @@
     group = first * NQ + s_z // NR
     stats = jnp.concatenate([x[:, :4] for x in (stats_o, stats_a, stats_b, stats_c)], axis=0)
     stats = stats.reshape(n_sec, 4 * row_dev)
-    choose = (group[:, None] == s[None, :]).astype(jnp.float32)
-    stats = jnp.dot(choose, stats, precision=lax.Precision.HIGHEST)
-    send = jnp.broadcast_to(stats[:, None, :], (n_sec, n_ten, 4 * row_dev))
-    send = send.reshape(n_sec * n_ten, 1, 4 * row_dev)
+    choose = (jnp.repeat(group, n_ten)[:, None] == s[None, :]).astype(jnp.float32)
+    send = jnp.dot(choose, stats, precision=lax.Precision.HIGHEST)[:, None, :]
     got = lax.all_to_all(send, PLANE, 0, 0).reshape(n_sec * n_ten, row_dev, 4)
 
     tops = got[:, :, 0]

time: 134 us -> 134 us (level)
  no operation moved by 1% of the time
where the time goes in v1:
time: 134 us
  starting transfers between devices  43.2 us (32%)
  blocking collectives  39.8 us (30%)
  waiting for transfers between devices  28.2 us (21%)
  Pallas kernels  11.2 us (8%)
  local copies, waits for them, and re-layouts  4.66 us (3%)
  other arithmetic  3.98 us (3%)
  between operations  1.59 us (1%)
    all_to_all x1, blocking collectives, per_device(): block = lax.all_to_all(block, ('zq', 'tensor'), 0, 0)  39.8 us
    ppermute x7, starting transfers between devices, fetch(): return lax.ppermute(x, PLANE, pairs)  34.9 us
    all_to_all x1, waiting for transfers between devices, per_device(): got = lax.all_to_all(send, PLANE, 0, 0).reshape(n_sec * n_ten, row_dev, 4)  15.1 us
    ppermute x7, waiting for transfers between devices, fetch(): return lax.ppermute(x, PLANE, pairs)  13.1 us
    pallas_call x4, Pallas kernels, stats_of(): pl.pallas_call(functools.partial(stats_kernel, len(rows), CHUNK), out_sha...  11.2 us
    all_to_all x1, starting transfers between devices, per_device(): got = lax.all_to_all(send, PLANE, 0, 0).reshape(n_sec * n_ten, row_dev, 4)  8.28 us
    unnamed x16, local copies, waits for them, and re-layouts  4.19 us
  transfers between devices with their start and end apart: 8, of which 4 were waited for; matrix products, arithmetic and copies ran while one was open for 1% of the time, Pallas kernels for 6%

profile of v1, /device:TPU:1, one launch (start us, length us, event | category | flops | bytes accessed | tf_op | source)
XLA Modules:
  0.0 133.6 jit_solution(13582365180238565885)
XLA Ops:
  0.6 0.7 fusion.20
  1.3 0.1 copy.39
  1.4 0.8 fusion.7
  2.2 39.8 %all_to_all.10 = bf16[16,8,2176]{2,1,0:T(8,128)(2,1)S(1)} all-to-all(bf16[16,8,2176]{2,1,0:T(8,128)(2,1)S(1)} %broadcast_in_dim.22), channel_id=1, replica_groups=mesh['y_lo'=2,'zq'=4,'zr'=3,'core'=2,'tensor'=4,'dp'=4] {'zq','tensor'}, dimensions={0} | all-to-all | bytes 1114112 | tf_op jit(solution)/shard_map/all_to_all | solution.py:109
  42.2 2.0 %collective-permute-start.2 = (bf16[32,8320]{1,0:T(8,128)(2,1)S(1)}, bf16[32,8320]{1,0:T(8,128)(2,1)S(1)}, u32[]{:S(2)}, u32[]{:S(2)}) collective-permute-start(bf16[32,8320]{1,0:T(8,128)(2,1)S(1)} %constant_dynamic-update-slice_fusion.refs_0_), channel_id=1, source_target_pairs={{384,0},{412,16},{416,32},{444,48},{448,64},{476,80},{480,96},{508... | collective-permute-start | bytes 1597448 | tf_op jit(solution)/shard_map/ppermute | solution.py:29
  44.1 13.6 %collective-permute-start.1 = (bf16[32,8320]{1,0:T(8,128)(2,1)S(1)}, bf16[32,8320]{1,0:T(8,128)(2,1)S(1)}, u32[]{:S(2)}, u32[]{:S(2)}) collective-permute-start(bf16[32,8320]{1,0:T(8,128)(2,1)S(1)} %constant_dynamic-update-slice_fusion.refs_0_), channel_id=1, source_target_pairs={{352,0},{368,16},{0,32},{16,48},{32,64},{48,80},{64,96},{80,112},{... | collective-permute-start | bytes 1597448 | tf_op jit(solution)/shard_map/ppermute | solution.py:29
  57.7 1.9 %collective-permute-start = (bf16[32,8320]{1,0:T(8,128)(2,1)S(1)}, bf16[32,8320]{1,0:T(8,128)(2,1)S(1)}, u32[]{:S(2)}, u32[]{:S(2)}) collective-permute-start(bf16[32,8320]{1,0:T(8,128)(2,1)S(1)} %constant_dynamic-update-slice_fusion.refs_0_), channel_id=1, source_target_pairs={{32,0},{48,16},{64,32},{80,48},{96,64},{112,80},{128,96},{144,112}... | collective-permute-start | bytes 1597448 | tf_op jit(solution)/shard_map/ppermute | solution.py:29
  59.7 0.0 collective-permute-done.2.refs_2_
  59.7 8.5 %collective-permute-done.1.refs_1_ = bf16[32,8320]{1,0:T(8,128)(2,1)S(1)} collective-permute-done((bf16[32,8320]{1,0:T(8,128)(2,1)S(1)}, bf16[32,8320]{1,0:T(8,128)(2,1)S(1)}, u32[]{:S(2)}, u32[]{:S(2)}) %collective-permute-start.1) | collective-permute-done | bytes 532512 | tf_op jit(solution)/shard_map/ppermute | solution.py:29
  68.2 3.8 %collective-permute-done.refs_0_ = bf16[32,8320]{1,0:T(8,128)(2,1)S(1)} collective-permute-done((bf16[32,8320]{1,0:T(8,128)(2,1)S(1)}, bf16[32,8320]{1,0:T(8,128)(2,1)S(1)}, u32[]{:S(2)}, u32[]{:S(2)}) %collective-permute-start) | collective-permute-done | bytes 532512 | tf_op jit(solution)/shard_map/ppermute | solution.py:29
  72.0 0.1 broadcast_select_fusion
  72.1 2.0 %collective-permute-start.5 = (bf16[32,8320]{1,0:T(8,128)(2,1)S(1)}, bf16[32,8320]{1,0:T(8,128)(2,1)S(1)}, u32[]{:S(2)}, u32[]{:S(2)}) collective-permute-start(bf16[32,8320]{1,0:T(8,128)(2,1)S(1)} %get-tuple-element.7), channel_id=1, source_target_pairs={{384,0},{368,16},{416,32},{16,48},{448,64},{48,80},{480,96},{80,11... | collective-permute-start | bytes 1597448 | tf_op jit(solution)/shard_map/ppermute | solution.py:29
  74.1 1.9 %collective-permute-start.4 = (bf16[32,8320]{1,0:T(8,128)(2,1)S(1)}, bf16[32,8320]{1,0:T(8,128)(2,1)S(1)}, u32[]{:S(2)}, u32[]{:S(2)}) collective-permute-start(bf16[32,8320]{1,0:T(8,128)(2,1)S(1)} %get-tuple-element.8), channel_id=1, source_target_pairs={{32,0},{412,16},{64,32},{444,48},{96,64},{476,80},{128,96},{508,11... | collective-permute-start | bytes 1597448 | tf_op jit(solution)/shard_map/ppermute | solution.py:29
  76.1 1.5 %pad_maximum_fusion = bf16[128,8320]{1,0:T(8,128)(2,1)} fusion(bf16[32,8320]{1,0:T(8,128)(2,1)S(1)} %collective-permute-done.2.refs_2_, bf16[32,8320]{1,0:T(8,128)(2,1)S(1)} %collective-permute-done.1.refs_1_, bf16[32,8320]{1,0:T(8,128)(2,1)S(1)} %collective-permute-done.refs_0_, bf16[32,8320]{1,0:T(8,128)(2,1)S(1)} %constant_dynamic-update-slice_fusion.refs_0_), kind=kLoop, calls=%fused_computation | loop fusion | flops 8519680 | bytes 4259840 | tf_op jit(solution)/shard_map/concatenate | solution.py:122
  77.6 8.0 %collective-permute-start.3 = (bf16[128,8320]{1,0:T(8,128)(2,1)}, bf16[128,8320]{1,0:T(8,128)(2,1)}, u32[]{:S(2)}, u32[]{:S(2)}) collective-permute-start(bf16[128,8320]{1,0:T(8,128)(2,1)} %pad_maximum_fusion), channel_id=1, source_target_pairs={{16,0},{0,16},{48,32},{32,48},{80,64},{64,80},{112,96},{96,112},{1... | collective-permute-start | bytes 6389768 | tf_op jit(solution)/shard_map/ppermute | solution.py:29
  85.6 0.7 collective-permute-done.4
  86.3 0.0 collective-permute-done.5
  86.4 5.5 %collective-permute-start.6 = (bf16[64,8320]{1,0:T(8,128)(2,1)S(1)}, bf16[64,8320]{1,0:T(8,128)(2,1)}, u32[]{:S(2)}, u32[]{:S(2)}) collective-permute-start(bf16[64,8320]{1,0:T(8,128)(2,1)S(1)} %constant_dynamic-update-slice_fusion.1.refs_0_), channel_id=1, source_target_pairs={{16,0},{0,16},{48,32},{32,48},{80,64},{64,80},{112,96},{96,112},{1... | collective-permute-start | bytes 3194888 | tf_op jit(solution)/shard_map/ppermute | solution.py:29
  92.0 0.1 broadcast_in_dim.21
  92.1 0.1 eq.34
  92.2 0.0 copy-start
  92.2 4.0 %copy-done = bf16[8192,640]{1,0:T(8,128)(2,1)S(1)} copy-done((bf16[8192,640]{1,0:T(8,128)(2,1)S(1)}, bf16[8192,640]{1,0:T(8,128)(2,1)}, u32[]{:S(2)}) %copy-start) | copy-done | bytes 10485784
  96.2 0.0 slice-start
  96.2 0.0 slice-start.1
  96.2 2.1 %shard_map.76 = f32[32,128]{1,0:T(8,128)S(1)} custom-call(s32[1]{0:T(128)} %bitcast.1.offset_ref, bf16[32,8320]{1,0:T(8,128)(2,1)S(1)} %constant_dynamic-update-slice_fusion.refs_0_, bf16[8192,640]{1,0:T(8,128)(2,1)S(1)} %copy-done), custom_call_target="tpu_custom_call" | custom-call | flops 335544320 | bytes 11010048 | tf_op jit(solution)/shard_map/pallas_call | solution.py:77
  98.3 0.0 slice-start.2
  98.3 2.1 %shard_map.77 = f32[96,128]{1,0:T(8,128)S(1)} custom-call(s32[1]{0:T(128)} %bitcast.1.offset_ref, bf16[32,8320]{1,0:T(8,128)(2,1)S(1)} %collective-permute-done.refs_0_, bf16[32,8320]{1,0:T(8,128)(2,1)S(1)} %collective-permute-done.1.refs_1_, bf16[32,8320]{1,0:T(8,128)(2,1)S(1)} %collective-permute-done.2.refs_2_, bf16[8192,640]{1,0:T(8,128)(2,1)S(1)} %copy-done), custom_call_target="tpu_custom_call" | custom-call | flops 1006632960 | bytes 12058624 | tf_op jit(solution)/shard_map/pallas_call | solution.py:77
  100.4 0.0 collective-permute-done.6.refs_1_
  100.4 0.0 slice-done
  100.5 0.0 slice-done.1
  100.5 0.0 slice-done.2
  100.5 3.3 %shard_map.79 = f32[128,128]{1,0:T(8,128)S(1)} custom-call(s32[1]{0:T(128)} %bitcast.1.offset_ref, bf16[64,8320]{1,0:T(8,128)(2,1)S(1)} %constant_dynamic-update-slice_fusion.1.refs_0_, bf16[64,8320]{1,0:T(8,128)(2,1)} %collective-permute-done.6.refs_1_, bf16[8192,640]{1,0:T(8,128)(2,1)S(1)} %bitcast.58), custom_call_target="tpu_custom_call" | custom-call | flops 1342177280 | bytes 12582912 | tf_op jit(solution)/shard_map/pallas_call | solution.py:77
  103.8 0.0 copy-start.1
  103.8 0.0 collective-permute-done.3.refs_0_
  103.8 3.7 %shard_map.78 = f32[128,128]{1,0:T(8,128)S(1)} custom-call(s32[1]{0:T(128)} %bitcast.1.offset_ref, bf16[128,8320]{1,0:T(8,128)(2,1)} %collective-permute-done.3.refs_0_, bf16[8192,640]{1,0:T(8,128)(2,1)S(1)} %bitcast.58), custom_call_target="tpu_custom_call" | custom-call | flops 1342177280 | bytes 12582912 | tf_op jit(solution)/shard_map/pallas_call | solution.py:77
  107.6 0.1 reshape.34
  107.7 0.9 fusion.4
  108.6 8.3 %all-to-all-start.1 = ((f32[192,1,32]{2,1,0:T(1,128)}), f32[192,1,32]{2,1,0:T(1,128)S(1)}, u32[]{:S(2)}, u32[]{:S(2)}) async-start(f32[192,1,32]{2,1,0:T(1,128)} %bitcast.15), calls=%async_computation.1 | async-start | bytes 196608 | tf_op jit(solution)/shard_map/all_to_all | solution.py:141
  117.5 15.1 %all-to-all-done.1 = f32[192,1,32]{2,1,0:T(1,128)S(1)} async-done(((f32[192,1,32]{2,1,0:T(1,128)}), f32[192,1,32]{2,1,0:T(1,128)S(1)}, u32[]{:S(2)}, u32[]{:S(2)}) %all-to-all-start.1) | async-done | bytes 24608 | tf_op jit(solution)/shard_map/all_to_all | solution.py:141
  132.6 0.1 copy.34
  132.7 0.2 fusion.26
  132.9 0.2 fusion.10
  133.1 0.0 copy-done.1
  133.1 0.5 subtract_select_fusion
  (13 shorter events, 0.3 us)
Async XLA Ops:
  42.2 17.5 %collective-permute-start.2 = (bf16[32,8320]{1,0:T(8,128)(2,1)S(1)}, bf16[32,8320]{1,0:T(8,128)(2,1)S(1)}, u32[]{:S(2)}, u32[]{:S(2)}) collective-permute-start(bf16[32,8320]{1,0:T(8,128)(2,1)S(1)} %constant_dynamic-update-slice_fusion.refs_0_), channel_id=1, source_target_pairs={{384,0},{412,16},{416,32},{444,48},{448,64},{476,80},{480,96},{508... | collective-permute-start | bytes 1597448 | tf_op jit(solution)/shard_map/ppermute | solution.py:29
  44.1 24.0 %collective-permute-start.1 = (bf16[32,8320]{1,0:T(8,128)(2,1)S(1)}, bf16[32,8320]{1,0:T(8,128)(2,1)S(1)}, u32[]{:S(2)}, u32[]{:S(2)}) collective-permute-start(bf16[32,8320]{1,0:T(8,128)(2,1)S(1)} %constant_dynamic-update-slice_fusion.refs_0_), channel_id=1, source_target_pairs={{352,0},{368,16},{0,32},{16,48},{32,64},{48,80},{64,96},{80,112},{... | collective-permute-start | bytes 1597448 | tf_op jit(solution)/shard_map/ppermute | solution.py:29
  57.7 14.3 %collective-permute-start = (bf16[32,8320]{1,0:T(8,128)(2,1)S(1)}, bf16[32,8320]{1,0:T(8,128)(2,1)S(1)}, u32[]{:S(2)}, u32[]{:S(2)}) collective-permute-start(bf16[32,8320]{1,0:T(8,128)(2,1)S(1)} %constant_dynamic-update-slice_fusion.refs_0_), channel_id=1, source_target_pairs={{32,0},{48,16},{64,32},{80,48},{96,64},{112,80},{128,96},{144,112}... | collective-permute-start | bytes 1597448 | tf_op jit(solution)/shard_map/ppermute | solution.py:29
  72.1 14.2 %collective-permute-start.5 = (bf16[32,8320]{1,0:T(8,128)(2,1)S(1)}, bf16[32,8320]{1,0:T(8,128)(2,1)S(1)}, u32[]{:S(2)}, u32[]{:S(2)}) collective-permute-start(bf16[32,8320]{1,0:T(8,128)(2,1)S(1)} %get-tuple-element.7), channel_id=1, source_target_pairs={{384,0},{368,16},{416,32},{16,48},{448,64},{48,80},{480,96},{80,11... | collective-permute-start | bytes 1597448 | tf_op jit(solution)/shard_map/ppermute | solution.py:29
  74.1 12.2 %collective-permute-start.4 = (bf16[32,8320]{1,0:T(8,128)(2,1)S(1)}, bf16[32,8320]{1,0:T(8,128)(2,1)S(1)}, u32[]{:S(2)}, u32[]{:S(2)}) collective-permute-start(bf16[32,8320]{1,0:T(8,128)(2,1)S(1)} %get-tuple-element.8), channel_id=1, source_target_pairs={{32,0},{412,16},{64,32},{444,48},{96,64},{476,80},{128,96},{508,11... | collective-permute-start | bytes 1597448 | tf_op jit(solution)/shard_map/ppermute | solution.py:29
  77.6 26.3 %collective-permute-start.3 = (bf16[128,8320]{1,0:T(8,128)(2,1)}, bf16[128,8320]{1,0:T(8,128)(2,1)}, u32[]{:S(2)}, u32[]{:S(2)}) collective-permute-start(bf16[128,8320]{1,0:T(8,128)(2,1)} %pad_maximum_fusion), channel_id=1, source_target_pairs={{16,0},{0,16},{48,32},{32,48},{80,64},{64,80},{112,96},{96,112},{1... | collective-permute-start | bytes 6389768 | tf_op jit(solution)/shard_map/ppermute | solution.py:29
  86.4 14.0 %collective-permute-start.6 = (bf16[64,8320]{1,0:T(8,128)(2,1)S(1)}, bf16[64,8320]{1,0:T(8,128)(2,1)}, u32[]{:S(2)}, u32[]{:S(2)}) collective-permute-start(bf16[64,8320]{1,0:T(8,128)(2,1)S(1)} %constant_dynamic-update-slice_fusion.1.refs_0_), channel_id=1, source_target_pairs={{16,0},{0,16},{48,32},{32,48},{80,64},{64,80},{112,96},{96,112},{1... | collective-permute-start | bytes 3194888 | tf_op jit(solution)/shard_map/ppermute | solution.py:29
  92.2 4.0 %copy-start = (bf16[8192,640]{1,0:T(8,128)(2,1)S(1)}, bf16[8192,640]{1,0:T(8,128)(2,1)}, u32[]{:S(2)}) copy-start(bf16[8192,640]{1,0:T(8,128)(2,1)} %refs_2_.1) | copy-start | bytes 31457284
  96.2 4.3 %slice-start = ((s8[10485760]{0:T(1024)(128)(4,1)}), s8[4194304]{0:T(1024)(128)(4,1)S(1)}, s32[]{:S(2)}) async-start(s8[10485760]{0:T(1024)(128)(4,1)} %bitcast.57), calls=%async_computation.2 | async-start | bytes 8388608
  96.2 4.3 %slice-start.1 = ((s8[10485760]{0:T(1024)(128)(4,1)}), s8[4194304]{0:T(1024)(128)(4,1)S(1)}, s32[]{:S(2)}) async-start(s8[10485760]{0:T(1024)(128)(4,1)} %bitcast.57), calls=%async_computation.3 | async-start | bytes 8388608
  98.3 2.2 %slice-start.2 = ((s8[10485760]{0:T(1024)(128)(4,1)}), s8[2097152]{0:T(1024)(128)(4,1)S(1)}, s32[]{:S(2)}) async-start(s8[10485760]{0:T(1024)(128)(4,1)} %bitcast.57), calls=%async_computation.4 | async-start | bytes 4194304
  103.8 29.3 %copy-start.1 = (f32[8]{0:T(128)S(1)}, f32[8]{0:T(128)}, u32[]{:S(2)}) copy-start(f32[8]{0:T(128)} %param.8) | copy-start | bytes 100
  108.6 24.1 %all-to-all-start.1 = ((f32[192,1,32]{2,1,0:T(1,128)}), f32[192,1,32]{2,1,0:T(1,128)S(1)}, u32[]{:S(2)}, u32[]{:S(2)}) async-start(f32[192,1,32]{2,1,0:T(1,128)} %bitcast.15), calls=%async_computation.1 | async-start | bytes 196608 | tf_op jit(solution)/shard_map/all_to_all | solution.py:141
